TPU v7x, 256 devices: a whole 4x4x8 slice. The times are simulated.
256 devices in a mesh: pair: 16 (over z_hi, y, core), aux: 16 (over x, z_lo).
Axes of the slice: x: 4, y: 4, z: 8 (z_hi: 2, z_lo: 4; z = z_hi * 4 + z_lo), core: 2. Of those that a mesh axis runs over, the one named last changes fastest.
Arguments:
- three_index: float32 [32, 768, 8192], P('pair', None, 'aux'), may hold values from -0.6 to 0.6
- occupied_energy: float32 [32], P('pair'), may hold values from -2 to -0.5
- virtual_energy: float32 [768], replicated, may hold values from 0.2 to 3
- plan: int32 [2, 32], P(None, 'pair'), may hold values from 0 to 1, as said below
Outputs:
- gradient_blocks: float32 [32, 768, 8192], P('pair', None, 'aux')
- virtual_density: float32 [768, 768], P('aux', 'pair')
Inputs may be any that keep to these rules, and one draw needn't show every extreme that they name: For block p and round r with q = p XOR 2**r: the row plan[r, p * 2 : (p + 1) * 2] is a permutation of the slots, and plan[r, q * 2 + plan[r, p * 2 + k]] = k, so every orbital is paired with exactly one orbital of block q in each round.
All inputs are finite; a program needn't handle non-finite values.
Results may differ from a plain program's by a relative error of at most 0.0001.
Values sent between devices are 32-bit elements; how exact they have to be, the bound alone decides.
A program may use at most 128 MiB of HBM per device.

v0:
```python
import jax
import jax.numpy as jnp
from jax import lax
from jax.sharding import PartitionSpec as P


def swapped(block, axis, bit):
    count = lax.axis_size(axis)
    route = []
    for low in range(count):
        high = low | 1 << bit
        if high != low and high < count:
            route += [(low, high), (high, low)]
    return lax.ppermute(block, axis, route)


def body(three_index, occupied_energy, virtual_energy, plan):
    highest = lax.Precision.HIGHEST
    per_block = three_index.shape[0]
    half_count = per_block // 2
    width = three_index.shape[1]
    row_count = width // lax.axis_size("aux")
    row_start = lax.axis_index("aux") * row_count
    position = lax.axis_index("pair")
    slots = jnp.arange(per_block, dtype=jnp.int32)
    lower_slots = slots[:half_count]
    upper_slots = slots[half_count:]
    gradient = jnp.zeros(three_index.shape, jnp.float32)
    density = jnp.zeros((row_count, width), jnp.float32)
    for turn_index in range(plan.shape[0]):
        table = plan[turn_index]
        upper_side = position // 2**turn_index % 2 == 1
        inverse = jnp.sum(jnp.where(table[None, :] == slots[:, None], slots[None, :], 0), axis=1)
        own_slots = jnp.where(upper_side, inverse[half_count:], lower_slots)
        peer_slots = jnp.where(upper_side, upper_slots, table[:half_count])
        send_slots = jnp.where(upper_side, inverse[:half_count], upper_slots)
        own_blocks = jnp.take(three_index, own_slots, axis=0)
        own_energy = jnp.take(occupied_energy, own_slots)
        peer_all, energy_all = swapped((three_index, occupied_energy), "pair", turn_index)
        peer_blocks = jnp.take(peer_all, peer_slots, axis=0)
        peer_energy = jnp.take(energy_all, peer_slots)
        pair_energy = own_energy + peer_energy
        partial_value = jnp.einsum(
            "hap,hbp->ahb",
            own_blocks,
            peer_blocks,
            precision=highest,
            preferred_element_type=jnp.float32,
        )
        summed = lax.psum(partial_value, "aux")
        gap_full = (
            pair_energy[None, :, None]
            - virtual_energy[:, None, None]
            - virtual_energy[None, None, :]
        )
        amplitude = summed / gap_full
        tilde = 2.0 * amplitude - jnp.transpose(amplitude, (2, 1, 0))
        amp_rows = lax.dynamic_slice_in_dim(amplitude, row_start, row_count, 0)
        amp_columns = lax.dynamic_slice_in_dim(amplitude, row_start, row_count, 2)
        density = density + jnp.einsum(
            "ahc,bhc->ab", amp_rows, tilde, precision=highest, preferred_element_type=jnp.float32
        )
        density = density + jnp.einsum(
            "cha,chb->ab", amp_columns, tilde, precision=highest, preferred_element_type=jnp.float32
        )
        own_term = jnp.einsum(
            "ahb,hbp->hap",
            tilde,
            peer_blocks,
            precision=highest,
            preferred_element_type=jnp.float32,
        )
        peer_term = jnp.einsum(
            "ahb,hap->hbp", tilde, own_blocks, precision=highest, preferred_element_type=jnp.float32
        )
        returned = swapped(peer_term, "pair", turn_index)
        gradient = gradient.at[own_slots].add(own_term)
        gradient = gradient.at[send_slots].add(returned)
    density = lax.psum_scatter(density, "pair", scatter_dimension=1, tiled=True)
    return (gradient, density)


def solution(mesh):
    in_specs = (P("pair", None, "aux"), P("pair"), P(), P(None, "pair"))
    out_specs = (P("pair", None, "aux"), P("aux", "pair"))
    return jax.shard_map(body, mesh=mesh, in_specs=in_specs, out_specs=out_specs, check_vma=False)
```

profile of v0, /device:TPU:1, one launch (start us, length us, event | category | flops | bytes accessed | tf_op | source)
XLA Modules:
  0.0 450.4 jit_solution(10524392798623498606)
XLA Ops:
  7.2 0.0 all-reduce.3.cloned.1.call-start
  7.2 3.3 collective-permute-start
  10.5 0.8 slice_bitcast_fusion
  11.3 0.1 fusion.86
  11.4 0.6 fusion.97
  12.7 0.6 slice.125
  13.3 1.3 fusion.94
  17.2 0.6 fusion.95
  18.5 0.0 copy-start.3
  18.5 7.9 %convolution_bitcast_fusion.1 = f32[768,1,768]{0,2,1:T(8,128)} fusion(f32[2,768,512]{2,1,0:T(8,128)S(1)} %collective-permute-done, s32[]{:T(128)} %bitcast.4, f32[2,768,512]{2,1,0:T(8,128)} %param.14, s32[]{:T(128)} %bitcast.7, pred[]{:T(512)} %bitcast.6, pred[]{:T(512)} %bitcast.3), kind=kOutput, calls=%fused_computation.24 | convolution fusion | flops 3624665088 | bytes 5507072 | tf_op jit(solution)/shard_map/hap,hbp->ahb/dot_general | solution.py:43
  26.5 53.9 %collective-permute-done.3 = f32[2,768,512]{2,1,0:T(8,128)} collective-permute-done((f32[2,768,512]{2,1,0:T(8,128)}, f32[2,768,512]{2,1,0:T(8,128)}, u32[]{:S(2)}, u32[]{:S(2)}) %collective-permute-start.3) | collective-permute-done | bytes 3145760 | tf_op jit(solution)/shard_map/ppermute | solution.py:14
  80.4 6.9 %convolution_bitcast_fusion = f32[768,1,768]{0,2,1:T(8,128)} fusion(f32[2,768,512]{2,1,0:T(8,128)} %collective-permute-done.3, s32[]{:T(128)} %bitcast.24, f32[2,768,512]{2,1,0:T(8,128)S(1)} %copy-done.3, s32[]{:T(128)} %bitcast.21, pred[]{:T(512)} %bitcast.26, pred[]{:T(512)} %bitcast.23), kind=kOutput, calls=%fused_computation.23 | convolution fusion | flops 3624665088 | bytes 5507072 | tf_op jit(solution)/shard_map/hap,hbp->ahb/dot_general | solution.py:43
  87.2 0.0 all-reduce.3.cloned.1.call-update
  87.3 0.0 reduce-scatter.4.cloned.1.call-start
  87.3 0.6 copy-done.9
  87.9 0.3 collective-permute-start.4
  88.2 1.4 collective-permute-start.1
  92.0 0.6 fusion.96
  93.8 0.8 and_reduce_fusion
  94.6 0.6 dynamic-slice.53
  95.8 0.6 dynamic-slice.51
  97.1 214.4 %all-reduce.3.cloned.1.call-done = (f32[768,1,768]{0,2,1:T(8,128)}, f32[768,1,768]{0,2,1:T(8,128)}) async-done(((f32[768,1,768]{0,2,1:T(8,128)}, f32[768,1,768]{0,2,1:T(8,128)}), (f32[768,1,768]{0,2,1:T(8,128)}, f32[768,1,768]{0,2,1:T(8,128)})) %all-reduce.3.cloned.1.call-update) | async-done | bytes 4718608 | tf_op jit(solution)/shard_map/psum | solution.py:50
  311.5 4.5 subtract_divide_fusion
  316.0 1.5 copy-done.2
  317.5 2.0 copy.10
  319.5 2.8 bitcast_subtract_fusion.1
  322.3 0.5 copy-done.4
  322.8 5.0 %fusion.27 = f32[1,768,512]{2,1,0:T(8,128)} fusion(f32[768,1,768]{2,0,1:T(8,128)S(1)} %bitcast_subtract_fusion.1, f32[2,768,512]{2,1,0:T(8,128)S(1)} %copy-done.4, s32[]{:T(128)} %bitcast.7, pred[]{:T(512)} %bitcast.6), kind=kOutput, calls=%fused_computation.41 | convolution fusion | flops 3624271872 | bytes 5505029 | tf_op jit(solution)/shard_map/ahb,hap->hbp/dot_general | solution.py:73
  327.8 1.2 collective-permute-start.2
  329.0 3.1 copy.11
  332.2 2.8 bitcast_subtract_fusion
  335.0 0.5 copy-done.5
  335.5 5.1 %fusion.32 = f32[1,768,512]{2,1,0:T(8,128)} fusion(f32[768,1,768]{2,0,1:T(8,128)S(1)} %bitcast_subtract_fusion, f32[2,768,512]{2,1,0:T(8,128)S(1)} %copy-done.5, s32[]{:T(128)} %bitcast.21, pred[]{:T(512)} %bitcast.26), kind=kOutput, calls=%fused_computation.42 | convolution fusion | flops 3624271872 | bytes 5505029 | tf_op jit(solution)/shard_map/ahb,hap->hbp/dot_general | solution.py:73
  340.6 1.4 collective-permute-start.5
  341.9 3.4 fusion.2
  345.3 2.4 fusion.8
  347.7 3.3 fusion.48
  351.1 2.4 fusion.51
  353.5 1.0 copy.12
  354.5 0.0 reduce-scatter.4.cloned.1.call-update
  354.5 2.1 broadcast_in_dim.57
  356.6 1.0 copy-done.7
  357.5 5.6 %bitcast_dynamic-update-slice_fusion = f32[2,768,512]{2,1,0:T(8,128)} fusion(f32[2,768,512]{2,1,0:T(8,128)} %broadcast_in_dim.57, s32[]{:T(128)} %bitcast.7, f32[768,1,768]{2,0,1:T(8,128)S(1)} %bitcast_subtract_fusion.1, f32[2,768,512]{2,1,0:T(8,128)S(1)} %copy-done.7, s32[]{:T(128)} %bitcast.4, pred[]{:T(512)} %bitcast.3, pred[]{:T(512)} %get-tuple-element.120), kind=kOutput, calls=%fused_computation.32 | convolution fusion | flops 3624665088 | bytes 5507072 | tf_op jit(solution)/shard_map/ahb,hbp->hap/dot_general | solution.py:66
  363.1 62.8 %reduce-scatter.4.cloned.1.call-done = f32[48,48]{1,0:T(8,128)} async-done(((f32[768,48]{1,0:T(8,128)}), f32[48,48]{1,0:T(8,128)}) %reduce-scatter.4.cloned.1.call-update) | async-done | bytes 9232
  425.9 1.4 copy.13
  427.4 4.2 fusion.16
  431.6 7.8 %fusion.17 = f32[2,768,512]{2,1,0:T(8,128)} fusion(f32[2,768,512]{2,1,0:T(8,128)} %fusion.16, s32[]{:T(128)} %bitcast.21, f32[2,768,512]{2,1,0:T(8,128)} %collective-permute-done.3, s32[]{:T(128)} %bitcast.24, f32[768,1,768]{2,0,1:T(8,128)S(1)} %copy-done.1, pred[]{:T(512)} %bitcast.23, pred[]{:T(512)} %get-tuple-element.107), kind=kOutput, calls=%fused_computation.26 | convolution fusion | flops 3625058304 | bytes 7079936 | tf_op jit(solution)/shard_map/ahb,hbp->hap/dot_general | solution.py:66
  439.4 4.0 fusion.18
  (25 shorter events, 0.1 us)
Async XLA Ops:
  7.2 304.3 %all-reduce.3.cloned.1.call-start = ((), (), s32[]{:S(2)}) async-start(), calls=%async_computation.2 | async-start | bytes 9437184 | tf_op jit(solution)/shard_map/psum | solution.py:50
  7.2 11.3 %collective-permute-start = (f32[2,768,512]{2,1,0:T(8,128)}, f32[2,768,512]{2,1,0:T(8,128)S(1)}, u32[]{:S(2)}, u32[]{:S(2)}) collective-permute-start(f32[2,768,512]{2,1,0:T(8,128)} %param.14), channel_id=1, source_target_pairs={{0,16},{16,0},{32,48},{48,32},{64,80},{80,64},{96,112},{112,96},{1... | collective-permute-start | bytes 9437192 | tf_op jit(solution)/shard_map/ppermute | solution.py:14
  10.5 69.9 %collective-permute-start.3 = (f32[2,768,512]{2,1,0:T(8,128)}, f32[2,768,512]{2,1,0:T(8,128)}, u32[]{:S(2)}, u32[]{:S(2)}) collective-permute-start(f32[2,768,512]{2,1,0:T(8,128)} %param.14), channel_id=1, source_target_pairs={{0,32},{32,0},{16,48},{48,16},{64,96},{96,64},{80,112},{112,80},{1... | collective-permute-start | bytes 9437192 | tf_op jit(solution)/shard_map/ppermute | solution.py:14
  18.5 8.0 %copy-start.6 = (f32[2,768,512]{2,1,0:T(8,128)}, f32[2,768,512]{2,1,0:T(8,128)S(1)}, u32[]{:S(2)}) copy-start(f32[2,768,512]{2,1,0:T(8,128)S(1)} %collective-permute-done) | copy-start | bytes 9437188
  18.5 61.8 %copy-start.3 = (f32[2,768,512]{2,1,0:T(8,128)S(1)}, f32[2,768,512]{2,1,0:T(8,128)}, u32[]{:S(2)}) copy-start(f32[2,768,512]{2,1,0:T(8,128)} %param.14) | copy-start | bytes 9437188
  87.2 0.7 copy-start.9
  87.2 6.5 %copy-start.10 = (s32[3]{0:T(128)S(1)}, s32[3]{0:T(128)}, u32[]{:S(2)}) copy-start(s32[3]{0:T(128)} %constant.173.clone.1) | copy-start | bytes 40
  87.2 9.9 %copy-start.8 = (f32[768]{0:T(1024)S(1)}, f32[768]{0:T(1024)}, u32[]{:S(2)}) copy-start(f32[768]{0:T(1024)} %param.16) | copy-start | bytes 9220
  87.3 338.7 %reduce-scatter.4.cloned.1.call-start = ((), (), s32[]{:S(2)}) async-start(), calls=%async_computation.1 | async-start | bytes 417792
  87.9 6.7 %collective-permute-start.4 = (f32[2]{0:T(128)S(1)}, f32[2]{0:T(128)S(1)}, u32[]{:S(2)}, u32[]{:S(2)}) collective-permute-start(f32[2]{0:T(128)S(1)} %copy-done.9), channel_id=1, source_target_pairs={{0,32},{32,0},{16,48},{48,16},{64,96},{96,64},{80,112},{112,80},{1... | collective-permute-start | bytes 32 | tf_op jit(solution)/shard_map/ppermute | solution.py:14
  88.2 7.7 %collective-permute-start.1 = (f32[2]{0:T(128)S(1)}, f32[2]{0:T(128)S(1)}, u32[]{:S(2)}, u32[]{:S(2)}) collective-permute-start(f32[2]{0:T(128)S(1)} %copy-done.9), channel_id=1, source_target_pairs={{0,16},{16,0},{32,48},{48,32},{64,80},{80,64},{96,112},{112,96},{1... | collective-permute-start | bytes 32 | tf_op jit(solution)/shard_map/ppermute | solution.py:14
  316.0 1.5 copy-start.2
  319.5 3.3 copy-start.4
  327.8 99.5 %collective-permute-start.2 = (f32[1,768,512]{2,1,0:T(8,128)}, f32[1,768,512]{2,1,0:T(8,128)}, u32[]{:S(2)}, u32[]{:S(2)}) collective-permute-start(f32[1,768,512]{2,1,0:T(8,128)} %fusion.27), channel_id=1, source_target_pairs={{0,16},{16,0},{32,48},{48,32},{64,80},{80,64},{96,112},{112,96},{1... | collective-permute-start | bytes 4718600 | tf_op jit(solution)/shard_map/ppermute | solution.py:14
  332.2 3.3 copy-start.5
  335.5 15.6 %copy-start = (f32[768,1,768]{2,0,1:T(8,128)}, f32[768,1,768]{2,0,1:T(8,128)S(1)}, u32[]{:S(2)}) copy-start(f32[768,1,768]{2,0,1:T(8,128)S(1)} %bitcast_subtract_fusion) | copy-start | bytes 7077892
  340.6 98.8 %collective-permute-start.5 = (f32[1,768,512]{2,1,0:T(8,128)}, f32[1,768,512]{2,1,0:T(8,128)}, u32[]{:S(2)}, u32[]{:S(2)}) collective-permute-start(f32[1,768,512]{2,1,0:T(8,128)} %fusion.32), channel_id=1, source_target_pairs={{0,32},{32,0},{16,48},{48,16},{64,96},{96,64},{80,112},{112,80},{1... | collective-permute-start | bytes 4718600 | tf_op jit(solution)/shard_map/ppermute | solution.py:14
  354.5 3.0 copy-start.7
  427.4 4.2 copy-start.1
Sparse Core Ops, SparseCore 0:
  87.4 224.0 all-reduce.2
  354.6 71.2 reduce-scatter.3
where the time goes:
time: 459 us; the launch traced here: 450 us
  waiting for transfers between devices  331 us (72%)
  matrix products  49.8 us (11%)
  between operations  23.3 us (5%)
  local copies, waits for them, and re-layouts  19.3 us (4%)
  other arithmetic  19.3 us (4%)
  starting transfers between devices  7.58 us (2%)
    psum x1, waiting for transfers between devices, body(): summed = lax.psum(partial_value, 'aux')  214 us
    unnamed x3, waiting for transfers between devices  62.9 us
    ppermute x6, waiting for transfers between devices, swapped(): return lax.ppermute(block, axis, route)  53.9 us
    dot_general x2, matrix products, body(): jnp.einsum('hap,hbp->ahb', own_blocks, peer_blocks, precision=highest, pr...  14.8 us
    dot_general x2, matrix products, body(): jnp.einsum('ahb,hbp->hap', tilde, peer_blocks, precision=highest, preferr...  13.4 us
    dot_general x2, matrix products, body(): jnp.einsum('ahb,hap->hbp', tilde, own_blocks, precision=highest, preferre...  10.1 us
  transfers between devices with their start and end apart: 8, of which 3 were waited for; matrix products, arithmetic and copies ran while one was open for 13% of the time, Pallas kernels for 0%

commit v1 on v0

v1 whole, which is shorter than its diff:
```python
import functools

import jax
import jax.numpy as jnp
from jax import lax
from jax.experimental import pallas as pl
from jax.experimental.pallas import tpu as pltpu
from jax.sharding import PartitionSpec as P

MESH = pl.DeviceIdType.MESH
F32 = jnp.float32
BF16 = jnp.bfloat16
V = 768
NP = 512
SUB = 48
HALF = SUB // 2
CHUNK = 4 * SUB
TILES = V // CHUNK
NN = (((1,), (0,)), ((), ()))
NT = (((1,), (1,)), ((), ()))


def split(value):
    high = value.astype(BF16)
    return high, (value - high.astype(F32)).astype(BF16)


def dot3(left, right, dims):
    (lh, ll), (rh, rl) = left, right

    def one(x, y):
        return lax.dot_general(x, y, dims, preferred_element_type=F32)

    return one(lh, rh) + (one(lh, rl) + one(ll, rh))


def rows(start, count):
    return pl.ds(pl.multiple_of(start, 8), count)


def kernel(
    b_hbm, occ, plan, virt, grad_hbm, dens_out,
    blk, bh, bl, sendb, peer, ph, plo, part, far_in, dir_in, acc, xsum, z_in, full, th, tl, uh, ul,
    rsend, rrecv, gown, outb, dt, d1, s1, d2, s2, d3,
    ld, ex, far, dirs, accs, zs, agz, agx, rel, ret, dsem, outs,
):
    p = lax.axis_index("pair")
    a = lax.axis_index("aux")
    core = p % 2
    y = (p // 2) % 4
    zh = p // 8
    x = a // 4
    z = a % 4

    def at_aux(xx, zz):
        return (p, (xx % 4) * 4 + zz % 4)

    def at_pair(hh, yy, cc):
        return (hh * 8 + (yy % 4) * 2 + cc, a)

    xdev = (at_aux(x + 1, z), at_aux(x + 3, z))
    chip_mate = at_pair(zh, y, 1 - core)
    y_mate = at_pair(zh, y + 1 - 2 * (y % 2), core)
    load = pltpu.make_async_copy(b_hbm, blk, ld)
    load.start()

    barrier = pltpu.get_barrier_semaphore()
    friends = [xdev[0], xdev[1], chip_mate, at_pair(1 - zh, y, core)]
    friends += [at_aux(x, z + j) for j in (1, 2, 3)]
    friends += [at_pair(zh, y + j, core) for j in (1, 2, 3)]
    for dev in friends:
        pl.semaphore_signal(barrier, inc=1, device_id=dev, device_id_type=MESH)

    def remote(src, dst, sems, index, dev):
        return pltpu.make_async_remote_copy(
            src_ref=src,
            dst_ref=dst,
            send_sem=sems.at[(0,) + index],
            recv_sem=sems.at[(1,) + index],
            device_id=dev,
            device_id_type=MESH,
        )

    sent = []

    def go(*args):
        copy = remote(*args)
        copy.start()
        sent.append(copy)

    def own_slot(r):
        upper = (p // (1 + r)) % 2
        return upper * (1 - plan[r, 0])

    def partner(r):
        return (p + (1 + r) - 2 * (1 + r) * ((p // (1 + r)) % 2), a)

    load.wait()

    def fill(r):
        other = 1 - own_slot(r)
        sendb[r, 0:V, :] = blk[other]
        sendb[r, V : V + 8, :] = jnp.full((8, NP), occ[other], F32)

    def exchange(r):
        go(sendb.at[r], peer.at[r], ex, (r,), partner(r))

    fill(0)
    fill(1)
    pl.semaphore_wait(barrier, len(friends))
    exchange(0)
    first_y = [None]

    def start_y():
        exchange(1)

    def split_own(i, carry):
        at = rows(i * CHUNK, CHUNK)
        for slot in range(2):
            high, low = split(blk[slot, at, :])
            bh[slot, at, :] = high
            bl[slot, at, :] = low
        return carry

    def part_chunk(r, c):
        at = rows((c % 4) * CHUNK, CHUNK)
        o = own_slot(r)
        part[r, at, :] = dot3((bh[o, at, :], bl[o, at, :]), (ph[r], plo[r]), NT)

    order = (1, 2, 3, 0)

    def integral(r):
        remote(sendb.at[r], peer.at[r], ex, (r,), partner(r)).wait_recv()

        def split_peer(i, carry):
            at = rows(i * CHUNK, CHUNK)
            high, low = split(peer[r, at, :])
            ph[r, at, :] = high
            plo[r, at, :] = low
            return carry

        lax.fori_loop(0, TILES, split_peer, 0)
        part_chunk(r, x + 2)
        for j in order:
            k = (z + j) % 4
            base = ((x + 2) % 4) * CHUNK + k * SUB
            for d in range(2):
                go(part.at[r, rows(base + d * HALF, HALF)], far_in.at[r, d, k], far, (r, d, k), xdev[d])
        part_chunk(r, x + 1)
        part_chunk(r, x + 3)
        for j in order:
            k = (z + j) % 4
            for d in range(2):
                base = ((x + 1 + 2 * d) % 4) * CHUNK + k * SUB + (1 - d) * HALF
                go(
                    part.at[r, rows(base, HALF)],
                    dir_in.at[r, d, k, pl.ds((1 - d) * HALF, HALF)],
                    dirs, (r, d, k), xdev[d],
                )
        part_chunk(r, x)

    def reduce(r):
        for j in order:
            k = (z + j) % 4
            for d in range(2):
                remote(far_in.at[r, d, k], far_in.at[r, d, k], far, (r, d, k), xdev[d]).wait_recv()
                base = ((x + 1 + 2 * d) % 4) * CHUNK + k * SUB + d * HALF
                acc[r, d, k] = part[r, rows(base, HALF), :] + far_in[r, d, k]
                go(acc.at[r, d, k], dir_in.at[r, d, k, pl.ds(d * HALF, HALF)], accs, (r, d, k), xdev[d])
        for j in order:
            k = (z + j) % 4
            for d in range(2):
                whole = dir_in.at[r, d, k]
                remote(
                    whole.at[pl.ds((1 - d) * HALF, HALF)], whole.at[pl.ds((1 - d) * HALF, HALF)],
                    dirs, (r, d, k), xdev[d],
                ).wait_recv()
                remote(acc.at[r, d, k], whole.at[pl.ds(d * HALF, HALF)], accs, (r, d, k), xdev[d]).wait_recv()
            xsum[r, k] = part[r, rows(x * CHUNK + k * SUB, SUB), :] + dir_in[r, 0, k] + dir_in[r, 1, k]
            if j:
                go(xsum.at[r, k], z_in.at[r, j - 1], zs, (r, j - 1), at_aux(x, z + j))
        total = xsum[r, z]
        for j in (1, 2, 3):
            remote(z_in.at[r, j - 1], z_in.at[r, j - 1], zs, (r, j - 1), at_aux(x, z + j)).wait_recv()
            total = total + z_in[r, j - 1]
        energy = occ[own_slot(r)] + peer[r, V : V + 1, 0:1]
        mine = rows(a * SUB, SUB)
        lane = lax.broadcasted_iota(jnp.int32, (SUB, V), 1)
        line = lax.broadcasted_iota(jnp.int32, (SUB, V), 0) + a * SUB
        level = jnp.sum(jnp.where(lane == line, virt[...], 0.0), axis=1, keepdims=True)
        full[r, mine, :] = total / ((energy - level) - virt[...])

    def block(r, xx, zz):
        return full.at[r, rows((xx % 4) * CHUNK + (zz % 4) * SUB, SUB)]

    def piece(r, xx, zz, d):
        return full.at[r, rows((xx % 4) * CHUNK + (zz % 4) * SUB + d * HALF, HALF)]

    def gather(r):
        mine = block(r, x, z)
        for d in range(2):
            go(mine, mine, agx, (r, d, z), xdev[d])
        for j in (1, 3, 2):
            go(mine, mine, agz, (r, j - 1), at_aux(x, z + j))
        for j in (1, 3, 2):
            got = block(r, x, z - j + 4)
            remote(got, got, agz, (r, j - 1), at_aux(x, z + j)).wait_recv()
            for d in range(2):
                go(got, got, agx, (r, d, (z - j + 4) % 4), xdev[d])
        for j in (0, 1, 3, 2):
            k = (z - j + 4) % 4
            for d in range(2):
                got = block(r, x + 3 - 2 * d, k)
                remote(got, got, agx, (r, d, k), xdev[d]).wait_recv()
                on = piece(r, x + 3 - 2 * d, k, d)
                go(on, on, rel, (r, d, k), xdev[d])
        for j in (0, 1, 3, 2):
            k = (z - j + 4) % 4
            for d in range(2):
                got = piece(r, x + 2, k, d)
                remote(got, got, rel, (r, d, k), xdev[d]).wait_recv()

    def tildes(r):
        def step(i, carry):
            at = pl.ds(pl.multiple_of(i * 128, 128), 128)
            here = full[r, at, :]
            there = full[r, :, at].T
            th[at, :], tl[at, :] = split(2.0 * here - there)
            uh[at, :], ul[at, :] = split(2.0 * there - here)
            return carry

        lax.fori_loop(0, V // 128, step, 0)

    def give_back(r):
        o = own_slot(r)

        def step(i, carry):
            at = rows(i * CHUNK, CHUNK)
            rsend[r, at, :] = dot3((uh[at, :], ul[at, :]), (bh[o], bl[o]), NN)
            return carry

        for i in range(TILES):
            step(i, 0)
            at = pl.ds(i * CHUNK, CHUNK)
            go(rsend.at[r, at], rrecv.at[r, at], ret, (r, i), partner(r))

    def keep(r):
        def step(i, carry):
            at = rows(i * CHUNK, CHUNK)
            gown[r, at, :] = dot3((th[at, :], tl[at, :]), (ph[r], plo[r]), NN)
            return carry

        lax.fori_loop(0, TILES, step, 0)

    def density(r, first):
        mine = rows(a * SUB, SUB)
        amp = full[r, mine, :]
        amp_t = 2.0 * amp - (th[mine, :].astype(F32) + tl[mine, :].astype(F32))
        pad = jnp.zeros((128 - SUB, V), F32)
        amp = split(jnp.concatenate([amp, pad], axis=0))
        amp_t = split(jnp.concatenate([amp_t, pad], axis=0))

        for i in range(TILES):
            at = pl.ds(i * CHUNK, CHUNK)
            value = dot3((th[at, :], tl[at, :]), amp, NT) + dot3((uh[at, :], ul[at, :]), amp_t, NT)
            value = value.reshape(2, 2, SUB, 128)
            if first:
                dt[2 * i : 2 * i + 2] = value
            else:
                dt[2 * i : 2 * i + 2] = dt[2 * i : 2 * i + 2] + value

    def spread():
        one = remote(dt.at[:, 1 - core], d1, dsem, (0,), chip_mate)
        one.start()
        one.wait_recv()
        s1[...] = dt[:, core] + d1[...]
        two = remote(s1.at[pl.ds(4 * (1 - zh), 4)], d2, dsem, (1,), at_pair(1 - zh, y, core))
        two.start()
        two.wait_recv()
        s2[...] = s1[pl.ds(4 * zh, 4)] + d2[...]
        three = [
            remote(s2.at[(y + j) % 4], d3.at[j - 1], dsem, (1 + j,), at_pair(zh, y + j, core)) for j in (1, 2, 3)
        ]
        for copy in three:
            copy.start()
        total = s2[y]
        for j in (1, 2, 3):
            three[j - 1].wait_recv()
            total = total + d3[j - 1]
        total = jnp.concatenate([total, jnp.zeros((128 - SUB, 128), F32)], axis=0).T
        dens_out[...] = total[0:SUB, 0:SUB]
        sent.extend([one, two] + three)

    early = 1 - core

    def first_round(t):
        return (t + early) % 2 if False else t

    lax.fori_loop(0, TILES, split_own, 0)
    start_y()
    for t in range(2):
        r = first_round(t)
        integral(r)
        reduce(r)
        gather(r)
        tildes(r)
        give_back(r)
        keep(r)
        density(r, t == 0)
    spread()

    o0 = own_slot(0)
    o1 = own_slot(1)
    writes = []
    for i in range(TILES):
        at = pl.ds(i * CHUNK, CHUNK)
        for r in range(2):
            remote(rsend.at[r, at], rrecv.at[r, at], ret, (r, i), partner(r)).wait_recv()
        k0, k1, n0, n1 = gown[0, at, :], gown[1, at, :], rrecv[0, at, :], rrecv[1, at, :]
        outb[0, at, :] = jnp.where(o0 == 0, k0, n0) + jnp.where(o1 == 0, k1, n1)
        outb[1, at, :] = jnp.where(o0 == 0, n0, k0) + jnp.where(o1 == 0, n1, k1)
        copy = pltpu.make_async_copy(outb.at[:, at], grad_hbm.at[:, at], outs.at[i])
        copy.start()
        writes.append(copy)
    for copy in sent:
        copy.wait_send()
    for copy in writes:
        copy.wait()


def body(three_index, occupied_energy, virtual_energy, plan):
    vm = pltpu.VMEM
    dma = pltpu.SemaphoreType.DMA
    return pl.pallas_call(
        kernel,
        out_shape=(
            jax.ShapeDtypeStruct((2, V, NP), F32),
            jax.ShapeDtypeStruct((SUB, SUB), F32),
        ),
        in_specs=[
            pl.BlockSpec(memory_space=pl.ANY),
            pl.BlockSpec(memory_space=pltpu.SMEM),
            pl.BlockSpec(memory_space=pltpu.SMEM),
            pl.BlockSpec(memory_space=pltpu.VMEM),
        ],
        out_specs=(pl.BlockSpec(memory_space=pl.ANY), pl.BlockSpec(memory_space=pltpu.VMEM)),
        scratch_shapes=[
            vm((2, V, NP), F32),
            vm((2, V, NP), BF16),
            vm((2, V, NP), BF16),
            vm((2, V + 8, NP), F32),
            vm((2, V + 8, NP), F32),
            vm((2, V, NP), BF16),
            vm((2, V, NP), BF16),
            vm((2, V, V), F32),
            vm((2, 2, 4, HALF, V), F32),
            vm((2, 2, 4, SUB, V), F32),
            vm((2, 2, 4, HALF, V), F32),
            vm((2, 4, SUB, V), F32),
            vm((2, 3, SUB, V), F32),
            vm((2, V, V), F32),
            vm((V, V), BF16),
            vm((V, V), BF16),
            vm((V, V), BF16),
            vm((V, V), BF16),
            vm((2, V, NP), F32),
            vm((2, V, NP), F32),
            vm((2, V, NP), F32),
            vm((2, V, NP), F32),
            vm((8, 2, SUB, 128), F32),
            vm((8, SUB, 128), F32),
            vm((8, SUB, 128), F32),
            vm((4, SUB, 128), F32),
            vm((4, SUB, 128), F32),
            vm((3, SUB, 128), F32),
            dma,
            dma((2, 2)),
            dma((2, 2, 2, 4)),
            dma((2, 2, 2, 4)),
            dma((2, 2, 2, 4)),
            dma((2, 2, 3)),
            dma((2, 2, 3)),
            dma((2, 2, 2, 4)),
            dma((2, 2, 2, 4)),
            dma((2, 2, TILES)),
            dma((2, 5)),
            dma((TILES,)),
        ],
        compiler_params=pltpu.CompilerParams(
            collective_id=0, has_side_effects=True, vmem_limit_bytes=64000 * 1024
        ),
        name="pairs",
    )(three_index, occupied_energy, plan, virtual_energy.reshape(1, V))


def solution(mesh):
    in_specs = (P("pair", None, "aux"), P("pair"), P(), P(None, "pair"))
    out_specs = (P("pair", None, "aux"), P("aux", "pair"))
    return jax.shard_map(body, mesh=mesh, in_specs=in_specs, out_specs=out_specs, check_vma=False)
```

time: 459 us -> 184 us (0.40)
  the two profiles are of different devices: /device:TPU:1 before, /device:TPU:32 now
where the time goes in v1:
time: 184 us
  Pallas kernels  178 us (97%)
  local copies, waits for them, and re-layouts  5.74 us (3%)
    pallas_call x1, Pallas kernels, body(): pl.pallas_call(kernel, out_shape=(jax.ShapeDtypeStruct((2, V, NP), F32),...  178 us
    unnamed x4, local copies, waits for them, and re-layouts  4.48 us

profile of v1, /device:TPU:32, one launch (start us, length us, event | category | flops | bytes accessed | tf_op | source)
XLA Modules:
  0.0 184.2 jit_solution(5858372325724423469)
XLA Ops:
  0.6 1.3 reshape.7.virt
  1.9 177.8 %pairs.1 = (f32[2,768,512]{2,1,0:T(8,128)}, f32[48,48]{1,0:T(8,128)}) custom-call(f32[2,768,512]{2,1,0:T(8,128)} %b_hbm.1, f32[2]{0:T(128)} %occ.1, s32[2,2]{1,0:T(2,128)} %plan.1, f32[1,768]{1,0:T(1,128)} %reshape.7.virt), custom_call_target="tpu_custom_call" | custom-call | tf_op jit(solution)/shard_map/pairs/pallas_call | solution.py:334
  179.7 0.0 copy-start
  179.7 3.9 %copy.8 = f32[2,768,512]{2,1,0:T(8,128)} copy(f32[2,768,512]{2,1,0:T(8,128)} %get-tuple-element.4) | data formatting | bytes 6291456
  183.6 0.0 copy-done
  183.6 0.6 copy.9
Async XLA Ops:
  179.7 3.9 %copy-start = (f32[48,48]{1,0:T(8,128)S(1)}, f32[48,48]{1,0:T(8,128)}, u32[]{:S(2)}) copy-start(f32[48,48]{1,0:T(8,128)} %get-tuple-element.5) | copy-start | bytes 27652

commit v2 on v1

--- a/solution.py
+++ b/solution.py
@@ -88,12 +88,14 @@
         copy.start()
         sent.append(copy)
 
+    def upper(r):
+        return core + r * (y % 2 - core)
+
     def own_slot(r):
-        upper = (p // (1 + r)) % 2
-        return upper * (1 - plan[r, 0])
+        return upper(r) * (1 - plan[r, 0])
 
     def partner(r):
-        return (p + (1 + r) - 2 * (1 + r) * ((p // (1 + r)) % 2), a)
+        return (p + (1 + r) * (1 - 2 * upper(r)), a)
 
     load.wait()
 
@@ -103,16 +105,17 @@
         sendb[r, V : V + 8, :] = jnp.full((8, NP), occ[other], F32)
 
     def exchange(r):
-        go(sendb.at[r], peer.at[r], ex, (r,), partner(r))
+        remote(sendb.at[r], peer.at[r], ex, (r,), partner(r)).start()
 
     fill(0)
     fill(1)
     pl.semaphore_wait(barrier, len(friends))
+
+    @pl.when(core == 0)
+    def _():
+        exchange(1)
+
     exchange(0)
-    first_y = [None]
-
-    def start_y():
-        exchange(1)
 
     def split_own(i, carry):
         at = rows(i * CHUNK, CHUNK)
@@ -159,7 +162,7 @@
                 )
         part_chunk(r, x)
 
-    def reduce(r):
+    def pass_on(r):
         for j in order:
             k = (z + j) % 4
             for d in range(2):
@@ -167,6 +170,8 @@
                 base = ((x + 1 + 2 * d) % 4) * CHUNK + k * SUB + d * HALF
                 acc[r, d, k] = part[r, rows(base, HALF), :] + far_in[r, d, k]
                 go(acc.at[r, d, k], dir_in.at[r, d, k, pl.ds(d * HALF, HALF)], accs, (r, d, k), xdev[d])
+
+    def across(r):
         for j in order:
             k = (z + j) % 4
             for d in range(2):
@@ -179,6 +184,8 @@
             xsum[r, k] = part[r, rows(x * CHUNK + k * SUB, SUB), :] + dir_in[r, 0, k] + dir_in[r, 1, k]
             if j:
                 go(xsum.at[r, k], z_in.at[r, j - 1], zs, (r, j - 1), at_aux(x, z + j))
+
+    def amplitude(r):
         total = xsum[r, z]
         for j in (1, 2, 3):
             remote(z_in.at[r, j - 1], z_in.at[r, j - 1], zs, (r, j - 1), at_aux(x, z + j)).wait_recv()
@@ -196,17 +203,24 @@
     def piece(r, xx, zz, d):
         return full.at[r, rows((xx % 4) * CHUNK + (zz % 4) * SUB + d * HALF, HALF)]
 
-    def gather(r):
+    def gather_z(r):
+        mine = block(r, x, z)
+        for j in (1, 3, 2):
+            go(mine, mine, agz, (r, j - 1), at_aux(x, z + j))
+
+    def gather_x(r):
         mine = block(r, x, z)
         for d in range(2):
             go(mine, mine, agx, (r, d, z), xdev[d])
-        for j in (1, 3, 2):
-            go(mine, mine, agz, (r, j - 1), at_aux(x, z + j))
+
+    def onward(r):
         for j in (1, 3, 2):
             got = block(r, x, z - j + 4)
             remote(got, got, agz, (r, j - 1), at_aux(x, z + j)).wait_recv()
             for d in range(2):
                 go(got, got, agx, (r, d, (z - j + 4) % 4), xdev[d])
+
+    def relay(r):
         for j in (0, 1, 3, 2):
             k = (z - j + 4) % 4
             for d in range(2):
@@ -214,6 +228,8 @@
                 remote(got, got, agx, (r, d, k), xdev[d]).wait_recv()
                 on = piece(r, x + 3 - 2 * d, k, d)
                 go(on, on, rel, (r, d, k), xdev[d])
+
+    def arrived(r):
         for j in (0, 1, 3, 2):
             k = (z - j + 4) % 4
             for d in range(2):
@@ -252,7 +268,7 @@
 
         lax.fori_loop(0, TILES, step, 0)
 
-    def density(r, first):
+    def density(r, first=False):
         mine = rows(a * SUB, SUB)
         amp = full[r, mine, :]
         amp_t = 2.0 * amp - (th[mine, :].astype(F32) + tl[mine, :].astype(F32))
@@ -291,41 +307,93 @@
         dens_out[...] = total[0:SUB, 0:SUB]
         sent.extend([one, two] + three)
 
-    early = 1 - core
-
-    def first_round(t):
-        return (t + early) % 2 if False else t
+    def finish():
+        o0 = own_slot(0)
+        o1 = own_slot(1)
+        writes = []
+        for i in range(TILES):
+            at = pl.ds(i * CHUNK, CHUNK)
+            for r in range(2):
+                remote(rsend.at[r, at], rrecv.at[r, at], ret, (r, i), partner(r)).wait_recv()
+            k0, k1, n0, n1 = gown[0, at, :], gown[1, at, :], rrecv[0, at, :], rrecv[1, at, :]
+            outb[0, at, :] = jnp.where(o0 == 0, k0, n0) + jnp.where(o1 == 0, k1, n1)
+            outb[1, at, :] = jnp.where(o0 == 0, n0, k0) + jnp.where(o1 == 0, n1, k1)
+            copy = pltpu.make_async_copy(outb.at[:, at], grad_hbm.at[:, at], outs.at[i])
+            copy.start()
+            writes.append(copy)
+        for r in range(2):
+            remote(sendb.at[r], peer.at[r], ex, (r,), partner(r)).wait_send()
+        for copy in sent:
+            copy.wait_send()
+        for copy in writes:
+            copy.wait()
 
     lax.fori_loop(0, TILES, split_own, 0)
-    start_y()
-    for t in range(2):
-        r = first_round(t)
-        integral(r)
-        reduce(r)
-        gather(r)
-        tildes(r)
-        give_back(r)
-        keep(r)
-        density(r, t == 0)
-    spread()
-
-    o0 = own_slot(0)
-    o1 = own_slot(1)
-    writes = []
-    for i in range(TILES):
-        at = pl.ds(i * CHUNK, CHUNK)
-        for r in range(2):
-            remote(rsend.at[r, at], rrecv.at[r, at], ret, (r, i), partner(r)).wait_recv()
-        k0, k1, n0, n1 = gown[0, at, :], gown[1, at, :], rrecv[0, at, :], rrecv[1, at, :]
-        outb[0, at, :] = jnp.where(o0 == 0, k0, n0) + jnp.where(o1 == 0, k1, n1)
-        outb[1, at, :] = jnp.where(o0 == 0, n0, k0) + jnp.where(o1 == 0, n1, k1)
-        copy = pltpu.make_async_copy(outb.at[:, at], grad_hbm.at[:, at], outs.at[i])
-        copy.start()
-        writes.append(copy)
-    for copy in sent:
-        copy.wait_send()
-    for copy in writes:
-        copy.wait()
+    integral(0)
+    pass_on(0)
+
+    @pl.when(core == 1)
+    def _():
+        exchange(1)
+
+    across(0)
+    amplitude(0)
+    gather_z(0)
+    before = list(sent)
+
+    @pl.when(core == 0)
+    def _():
+        sent[:] = before
+        integral(1)
+        pass_on(1)
+        gather_x(0)
+        across(1)
+        onward(0)
+        amplitude(1)
+        gather_z(1)
+        gather_x(1)
+        onward(1)
+        relay(1)
+        relay(0)
+        arrived(1)
+        tildes(1)
+        give_back(1)
+        arrived(0)
+        keep(1)
+        density(1, True)
+        tildes(0)
+        give_back(0)
+        keep(0)
+        density(0)
+        spread()
+        finish()
+
+    @pl.when(core == 1)
+    def _():
+        sent[:] = before
+        gather_x(0)
+        onward(0)
+        relay(0)
+        integral(1)
+        arrived(0)
+        pass_on(1)
+        tildes(0)
+        give_back(0)
+        across(1)
+        keep(0)
+        amplitude(1)
+        gather_z(1)
+        gather_x(1)
+        density(0, True)
+        onward(1)
+        relay(1)
+        arrived(1)
+        tildes(1)
+        give_back(1)
+        keep(1)
+        density(1)
+        spread()
+        finish()
 
 
 def body(three_index, occupied_energy, virtual_energy, plan):

time: 184 us -> 146 us (0.79)
  the two profiles are of different devices: /device:TPU:32 before, /device:TPU:1 now
where the time goes in v2:
time: 146 us
  Pallas kernels  140 us (96%)
  local copies, waits for them, and re-layouts  5.74 us (4%)
    pallas_call x1, Pallas kernels, body(): pl.pallas_call(kernel, out_shape=(jax.ShapeDtypeStruct((2, V, NP), F32),...  140 us
    unnamed x4, local copies, waits for them, and re-layouts  4.48 us

profile of v2, /device:TPU:1, one launch (start us, length us, event | category | flops | bytes accessed | tf_op | source)
XLA Modules:
  0.0 146.1 jit_solution(16419184911725103317)
XLA Ops:
  0.6 1.3 reshape.7.virt
  1.9 139.7 %pairs.1 = (f32[2,768,512]{2,1,0:T(8,128)}, f32[48,48]{1,0:T(8,128)}) custom-call(f32[2,768,512]{2,1,0:T(8,128)} %b_hbm.1, f32[2]{0:T(128)} %occ.1, s32[2,2]{1,0:T(2,128)} %plan.1, f32[1,768]{1,0:T(1,128)} %reshape.7.virt), custom_call_target="tpu_custom_call" | custom-call | tf_op jit(solution)/shard_map/pairs/pallas_call | solution.py:402
  141.6 0.0 copy-start
  141.6 3.9 %copy.8 = f32[2,768,512]{2,1,0:T(8,128)} copy(f32[2,768,512]{2,1,0:T(8,128)} %get-tuple-element.4) | data formatting | bytes 6291456
  145.5 0.0 copy-done
  145.5 0.6 copy.9
Async XLA Ops:
  141.6 3.9 %copy-start = (f32[48,48]{1,0:T(8,128)S(1)}, f32[48,48]{1,0:T(8,128)}, u32[]{:S(2)}) copy-start(f32[48,48]{1,0:T(8,128)} %get-tuple-element.5) | copy-start | bytes 27652

commit v3 on v2

--- a/solution.py
+++ b/solution.py
@@ -41,8 +41,8 @@
 def kernel(
     b_hbm, occ, plan, virt, grad_hbm, dens_out,
     blk, bh, bl, sendb, peer, ph, plo, part, far_in, dir_in, acc, xsum, z_in, full, th, tl, uh, ul,
-    rsend, rrecv, gown, outb, dt, d1, s1, d2, s2, d3,
-    ld, ex, far, dirs, accs, zs, agz, agx, rel, ret, dsem, outs,
+    rsend, rrecv, gown, dt, d1, s1, d2, s2, d3,
+    ld, ex, far, dirs, accs, zs, agc, agd, agx, rel, ret, dsem, outs,
 ):
     p = lax.axis_index("pair")
     a = lax.axis_index("aux")
@@ -59,6 +59,8 @@
         return (hh * 8 + (yy % 4) * 2 + cc, a)
 
     xdev = (at_aux(x + 1, z), at_aux(x + 3, z))
+    zdev = (at_aux(x, z + 1), at_aux(x, z + 3))
+    ends = (3, 0)
     chip_mate = at_pair(zh, y, 1 - core)
     y_mate = at_pair(zh, y + 1 - 2 * (y % 2), core)
     load = pltpu.make_async_copy(b_hbm, blk, ld)
@@ -194,8 +196,9 @@
         mine = rows(a * SUB, SUB)
         lane = lax.broadcasted_iota(jnp.int32, (SUB, V), 1)
         line = lax.broadcasted_iota(jnp.int32, (SUB, V), 0) + a * SUB
-        level = jnp.sum(jnp.where(lane == line, virt[...], 0.0), axis=1, keepdims=True)
-        full[r, mine, :] = total / ((energy - level) - virt[...])
+        across_v = virt[...].reshape(1, V)
+        level = jnp.sum(jnp.where(lane == line, across_v, 0.0), axis=1, keepdims=True)
+        full[r, mine, :] = total / ((energy - level) - across_v)
 
     def block(r, xx, zz):
         return full.at[r, rows((xx % 4) * CHUNK + (zz % 4) * SUB, SUB)]
@@ -203,31 +206,67 @@
     def piece(r, xx, zz, d):
         return full.at[r, rows((xx % 4) * CHUNK + (zz % 4) * SUB + d * HALF, HALF)]
 
+    def ring_block(r, d, k):
+        return remote(block(r, x, k), block(r, x, k), agx, (r, d, k), xdev[d])
+
+    def straight(r, j):
+        mine = block(r, x, z)
+        return remote(mine, mine, agd, (r, j - 1), at_aux(x, z + j))
+
     def gather_z(r):
-        mine = block(r, x, z)
         for j in (1, 3, 2):
-            go(mine, mine, agz, (r, j - 1), at_aux(x, z + j))
+            straight(r, j).start()
 
     def gather_x(r):
-        mine = block(r, x, z)
         for d in range(2):
-            go(mine, mine, agx, (r, d, z), xdev[d])
-
-    def onward(r):
-        for j in (1, 3, 2):
-            got = block(r, x, z - j + 4)
-            remote(got, got, agz, (r, j - 1), at_aux(x, z + j)).wait_recv()
-            for d in range(2):
-                go(got, got, agx, (r, d, (z - j + 4) % 4), xdev[d])
-
-    def relay(r):
-        for j in (0, 1, 3, 2):
-            k = (z - j + 4) % 4
+            ring_block(r, d, z).start()
+
+    def onward(r, *which):
+        for i in which:
+            k = (z - i + 4) % 4
+            got = block(r, x, k)
+            remote(got, got, agd, (r, i - 1), at_aux(x, z + i)).wait_recv()
+            for e in range(2):
+                ring_block(r, e, k).start()
+
+    def ring_relay(r, d, k):
+        on = piece(r, x + 3 - 2 * d, k, d)
+        return remote(on, on, rel, (r, d, k), xdev[d])
+
+    def relay(r, *which):
+        for i in which:
+            k = (z - i + 4) % 4
             for d in range(2):
                 got = block(r, x + 3 - 2 * d, k)
                 remote(got, got, agx, (r, d, k), xdev[d]).wait_recv()
-                on = piece(r, x + 3 - 2 * d, k, d)
-                go(on, on, rel, (r, d, k), xdev[d])
+                ring_relay(r, d, k).start()
+
+    def column(d, k, xx):
+        return remote(block(0, xx, k), block(0, xx, k), agc, (d, k, xx), zdev[d])
+
+    def ring_first():
+        for d in range(2):
+            got = piece(0, x + 2, z, d)
+            remote(got, got, rel, (0, d, z), xdev[d]).wait_recv()
+        for d in range(2):
+            @pl.when(z != ends[d])
+            def _(d=d):
+                for xx in range(4):
+                    column(d, z, xx).start()
+
+    def hop(*which):
+        for i in which:
+            for d in range(2):
+                k = z - i * (1 - 2 * d)
+
+                @pl.when((k >= 0) & (k <= 3))
+                def _(d=d, k=k):
+                    for xx in range(4):
+                        column(d, k, xx).wait_recv()
+
+                        @pl.when(z != ends[d])
+                        def _():
+                            column(d, k, xx).start()
 
     def arrived(r):
         for j in (0, 1, 3, 2):
@@ -247,17 +286,11 @@
 
         lax.fori_loop(0, V // 128, step, 0)
 
-    def give_back(r):
+    def give_back(r, first=0, last=TILES):
         o = own_slot(r)
-
-        def step(i, carry):
-            at = rows(i * CHUNK, CHUNK)
+        for i in range(first, last):
+            at = pl.ds(i * CHUNK, CHUNK)
             rsend[r, at, :] = dot3((uh[at, :], ul[at, :]), (bh[o], bl[o]), NN)
-            return carry
-
-        for i in range(TILES):
-            step(i, 0)
-            at = pl.ds(i * CHUNK, CHUNK)
             go(rsend.at[r, at], rrecv.at[r, at], ret, (r, i), partner(r))
 
     def keep(r):
@@ -285,29 +318,38 @@
             else:
                 dt[2 * i : 2 * i + 2] = dt[2 * i : 2 * i + 2] + value
 
-    def spread():
-        one = remote(dt.at[:, 1 - core], d1, dsem, (0,), chip_mate)
-        one.start()
-        one.wait_recv()
-        s1[...] = dt[:, core] + d1[...]
-        two = remote(s1.at[pl.ds(4 * (1 - zh), 4)], d2, dsem, (1,), at_pair(1 - zh, y, core))
-        two.start()
-        two.wait_recv()
-        s2[...] = s1[pl.ds(4 * zh, 4)] + d2[...]
-        three = [
-            remote(s2.at[(y + j) % 4], d3.at[j - 1], dsem, (1 + j,), at_pair(zh, y + j, core)) for j in (1, 2, 3)
-        ]
-        for copy in three:
-            copy.start()
+    def column_copies():
+        return [remote(s2.at[(y + j) % 4], d3.at[j - 1], dsem, (1 + j,), at_pair(zh, y + j, core)) for j in (1, 2, 3)]
+
+    def chip_copy():
+        return remote(dt.at[:, 1 - core], d1, dsem, (0,), chip_mate)
+
+    def far_copy():
+        return remote(s1.at[pl.ds(4 * (1 - zh), 4)], d2, dsem, (1,), at_pair(1 - zh, y, core))
+
+    def spread(stage):
+        if stage == 0:
+            chip_copy().start()
+        if stage == 1:
+            chip_copy().wait_recv()
+            s1[...] = dt[:, core] + d1[...]
+            far_copy().start()
+        if stage == 2:
+            far_copy().wait_recv()
+            s2[...] = s1[pl.ds(4 * zh, 4)] + d2[...]
+            for copy in column_copies():
+                copy.start()
+
+    def settle():
         total = s2[y]
-        for j in (1, 2, 3):
-            three[j - 1].wait_recv()
-            total = total + d3[j - 1]
+        for j, copy in enumerate(column_copies()):
+            copy.wait_recv()
+            total = total + d3[j]
         total = jnp.concatenate([total, jnp.zeros((128 - SUB, 128), F32)], axis=0).T
         dens_out[...] = total[0:SUB, 0:SUB]
-        sent.extend([one, two] + three)
-
-    def finish():
+        sent.extend([chip_copy(), far_copy()] + column_copies())
+
+    def finish(columns):
         o0 = own_slot(0)
         o1 = own_slot(1)
         writes = []
@@ -316,84 +358,119 @@
             for r in range(2):
                 remote(rsend.at[r, at], rrecv.at[r, at], ret, (r, i), partner(r)).wait_recv()
             k0, k1, n0, n1 = gown[0, at, :], gown[1, at, :], rrecv[0, at, :], rrecv[1, at, :]
-            outb[0, at, :] = jnp.where(o0 == 0, k0, n0) + jnp.where(o1 == 0, k1, n1)
-            outb[1, at, :] = jnp.where(o0 == 0, n0, k0) + jnp.where(o1 == 0, n1, k1)
-            copy = pltpu.make_async_copy(outb.at[:, at], grad_hbm.at[:, at], outs.at[i])
+            gown[0, at, :] = jnp.where(o0 == 0, k0, n0) + jnp.where(o1 == 0, k1, n1)
+            gown[1, at, :] = jnp.where(o0 == 0, n0, k0) + jnp.where(o1 == 0, n1, k1)
+            copy = pltpu.make_async_copy(gown.at[:, at], grad_hbm.at[:, at], outs.at[i])
             copy.start()
             writes.append(copy)
+            if i == 0:
+                spread(2)
+        settle()
         for r in range(2):
             remote(sendb.at[r], peer.at[r], ex, (r,), partner(r)).wait_send()
         for copy in sent:
             copy.wait_send()
+        for r in range(2):
+            if r == 0 and columns:
+                continue
+            for j in (1, 2, 3):
+                straight(r, j).wait_send()
+            for k in range(4):
+                for d in range(2):
+                    ring_block(r, d, k).wait_send()
+                    ring_relay(r, d, k).wait_send()
+        if columns:
+            for d in range(2):
+                ring_block(0, d, z).wait_send()
+                ring_relay(0, d, z).wait_send()
+                for k in range(4):
+                    @pl.when(((z - k) * (1 - 2 * d) >= 0) & (z != ends[d]))
+                    def _(d=d, k=k):
+                        for xx in range(4):
+                            column(d, k, xx).wait_send()
         for copy in writes:
             copy.wait()
 
     lax.fori_loop(0, TILES, split_own, 0)
     integral(0)
     pass_on(0)
-
-    @pl.when(core == 1)
-    def _():
-        exchange(1)
-
-    across(0)
-    amplitude(0)
-    gather_z(0)
     before = list(sent)
 
     @pl.when(core == 0)
     def _():
         sent[:] = before
         integral(1)
+        across(0)
         pass_on(1)
-        gather_x(0)
         across(1)
-        onward(0)
         amplitude(1)
         gather_z(1)
         gather_x(1)
-        onward(1)
-        relay(1)
-        relay(0)
+        amplitude(0)
+        onward(1, 1)
+        relay(1, 0)
+        onward(1, 3)
+        relay(1, 1)
+        onward(1, 2)
+        relay(1, 3)
+        relay(1, 2)
+        arrived(1)
+        gather_z(0)
+        tildes(1)
+        give_back(1)
+        keep(1)
+        density(1, True)
+        gather_x(0)
+        onward(0, 1, 3, 2)
+        relay(0, 0)
+        relay(0, 1)
+        relay(0, 3, 2)
+        arrived(0)
+        tildes(0)
+        density(0)
+        spread(0)
+        give_back(0)
+        keep(0)
+        spread(1)
+        finish(False)
+
+    @pl.when(core == 1)
+    def _():
+        sent[:] = before
+        exchange(1)
+        across(0)
+        amplitude(0)
+        gather_x(0)
+        integral(1)
+        relay(0, 0)
+        pass_on(1)
+        across(1)
+        amplitude(1)
+        gather_z(1)
+        gather_x(1)
+        onward(1, 1)
+        relay(1, 0)
+        onward(1, 3)
+        relay(1, 1)
+        onward(1, 2)
+        ring_first()
+        relay(1, 3)
+        relay(1, 2)
         arrived(1)
         tildes(1)
         give_back(1)
-        arrived(0)
+        hop(1)
         keep(1)
+        hop(2)
         density(1, True)
+        hop(3)
         tildes(0)
+        density(0)
+        spread(0)
         give_back(0)
         keep(0)
-        density(0)
-        spread()
-        finish()
-
-    @pl.when(core == 1)
-    def _():
-        sent[:] = before
-        gather_x(0)
-        onward(0)
-        relay(0)
-        integral(1)
-        arrived(0)
-        pass_on(1)
-        tildes(0)
-        give_back(0)
-        across(1)
-        keep(0)
-        amplitude(1)
-        gather_z(1)
-        gather_x(1)
-        density(0, True)
-        onward(1)
-        relay(1)
-        arrived(1)
-        tildes(1)
-        give_back(1)
-        keep(1)
-        density(1)
-        spread()
-        finish()
+        spread(1)
+        finish(True)
 
 
 def body(three_index, occupied_energy, virtual_energy, plan):
@@ -434,7 +511,6 @@
             vm((2, V, NP), F32),
             vm((2, V, NP), F32),
             vm((2, V, NP), F32),
-            vm((2, V, NP), F32),
             vm((8, 2, SUB, 128), F32),
             vm((8, SUB, 128), F32),
             vm((8, SUB, 128), F32),
@@ -447,6 +523,7 @@
             dma((2, 2, 2, 4)),
             dma((2, 2, 2, 4)),
             dma((2, 2, 3)),
+            dma((2, 2, 4, 4)),
             dma((2, 2, 3)),
             dma((2, 2, 2, 4)),
             dma((2, 2, 2, 4)),
@@ -455,10 +532,10 @@
             dma((TILES,)),
         ],
         compiler_params=pltpu.CompilerParams(
-            collective_id=0, has_side_effects=True, vmem_limit_bytes=64000 * 1024
+            collective_id=0, has_side_effects=True, vmem_limit_bytes=50 * 1024 * 1024
         ),
         name="pairs",
-    )(three_index, occupied_energy, plan, virtual_energy.reshape(1, V))
+    )(three_index, occupied_energy, plan, virtual_energy)
 
 
 def solution(mesh):

time: 146 us -> 132 us (0.904)
  Pallas kernels: 140 us -> 127 us
    pallas_call x1, Pallas kernels: 140 us -> 127 us  [body(): pl.pallas_call(kernel, out_shape=(jax.ShapeDtypeStruct((2, V, NP), F32),...]
    unnamed x4 -> x8, local copies, waits for them, and re-layouts: 4.48 us -> 4.29 us
where the time goes in v3:
time: 132 us
  Pallas kernels  127 us (96%)
  local copies, waits for them, and re-layouts  4.29 us (3%)
    pallas_call x1, Pallas kernels, body(): pl.pallas_call(kernel, out_shape=(jax.ShapeDtypeStruct((2, V, NP), F32),...  127 us
    unnamed x8, local copies, waits for them, and re-layouts  4.29 us

profile of v3, /device:TPU:1, one launch (start us, length us, event | category | flops | bytes accessed | tf_op | source)
XLA Modules:
  0.0 131.8 jit_solution(5996446166390031615)
XLA Ops:
  0.6 0.0 copy-start
  0.6 0.7 copy-done
  1.3 0.0 copy-start.1
  1.3 0.7 copy-done.1
  2.0 0.0 copy-start.2
  2.0 0.7 copy-done.2
  2.7 126.9 %pairs.1 = (f32[2,768,512]{2,1,0:T(8,128)S(1)}, f32[48,48]{1,0:T(8,128)S(1)}) custom-call(f32[2,768,512]{2,1,0:T(8,128)} %b_hbm.1, f32[2]{0:T(128)S(1)} %copy-done.2, s32[2,2]{1,0:T(2,128)S(1)} %copy-done.1, f32[768]{0:T(1024)S(1)} %copy-done), custom_call_target="tpu_custom_call" | custom-call | tf_op jit(solution)/shard_map/pairs/pallas_call | solution.py:479
  129.5 1.7 %copy.8 = f32[2,768,512]{2,1,0:T(8,128)} copy(f32[2,768,512]{2,1,0:T(8,128)S(1)} %get-tuple-element.4) | data formatting | bytes 6291456
  131.2 0.6 copy.9
Async XLA Ops:
  0.6 0.7 copy-start
  1.3 0.7 copy-start.1
  2.0 0.7 copy-start.2

commit v4 on v3

--- a/solution.py
+++ b/solution.py
@@ -42,7 +42,7 @@
     b_hbm, occ, plan, virt, grad_hbm, dens_out,
     blk, bh, bl, sendb, peer, ph, plo, part, far_in, dir_in, acc, xsum, z_in, full, th, tl, uh, ul,
     rsend, rrecv, gown, dt, d1, s1, d2, s2, d3,
-    ld, ex, far, dirs, accs, zs, agc, agd, agx, rel, ret, dsem, outs,
+    ld, ex, far, dirs, accs, zs, agd, agx, rel, ret, dsem, outs,
 ):
     p = lax.axis_index("pair")
     a = lax.axis_index("aux")
@@ -59,8 +59,6 @@
         return (hh * 8 + (yy % 4) * 2 + cc, a)
 
     xdev = (at_aux(x + 1, z), at_aux(x + 3, z))
-    zdev = (at_aux(x, z + 1), at_aux(x, z + 3))
-    ends = (3, 0)
     chip_mate = at_pair(zh, y, 1 - core)
     y_mate = at_pair(zh, y + 1 - 2 * (y % 2), core)
     load = pltpu.make_async_copy(b_hbm, blk, ld)
@@ -106,8 +104,15 @@
         sendb[r, 0:V, :] = blk[other]
         sendb[r, V : V + 8, :] = jnp.full((8, NP), occ[other], F32)
 
+    chunks = (2, 1, 3, 0)
+
+    def row_chunk(r, i):
+        at = rows(((x + chunks[i]) % 4) * CHUNK, CHUNK) if i < 4 else pl.ds(V, 8)
+        return remote(sendb.at[r, at], peer.at[r, at], ex, (r, i), partner(r))
+
     def exchange(r):
-        remote(sendb.at[r], peer.at[r], ex, (r,), partner(r)).start()
+        for i in (4, 0, 1, 2, 3):
+            row_chunk(r, i).start()
 
     fill(0)
     fill(1)
@@ -127,42 +132,33 @@
             bl[slot, at, :] = low
         return carry
 
-    def part_chunk(r, c):
-        at = rows((c % 4) * CHUNK, CHUNK)
-        o = own_slot(r)
-        part[r, at, :] = dot3((bh[o, at, :], bl[o, at, :]), (ph[r], plo[r]), NT)
-
-    order = (1, 2, 3, 0)
-
-    def integral(r):
-        remote(sendb.at[r], peer.at[r], ex, (r,), partner(r)).wait_recv()
-
-        def split_peer(i, carry):
-            at = rows(i * CHUNK, CHUNK)
+    order = (2, 3, 1, 0)
+
+    def integral(r, *which):
+        for i in which:
+            if i == 0:
+                row_chunk(r, 4).wait_recv()
+            row_chunk(r, i).wait_recv()
+            c = (x + chunks[i]) % 4
+            at = rows(c * CHUNK, CHUNK)
+            o = own_slot(r)
             high, low = split(peer[r, at, :])
             ph[r, at, :] = high
             plo[r, at, :] = low
-            return carry
-
-        lax.fori_loop(0, TILES, split_peer, 0)
-        part_chunk(r, x + 2)
-        for j in order:
-            k = (z + j) % 4
-            base = ((x + 2) % 4) * CHUNK + k * SUB
-            for d in range(2):
-                go(part.at[r, rows(base + d * HALF, HALF)], far_in.at[r, d, k], far, (r, d, k), xdev[d])
-        part_chunk(r, x + 1)
-        part_chunk(r, x + 3)
-        for j in order:
-            k = (z + j) % 4
-            for d in range(2):
-                base = ((x + 1 + 2 * d) % 4) * CHUNK + k * SUB + (1 - d) * HALF
-                go(
-                    part.at[r, rows(base, HALF)],
-                    dir_in.at[r, d, k, pl.ds((1 - d) * HALF, HALF)],
-                    dirs, (r, d, k), xdev[d],
-                )
-        part_chunk(r, x)
+            part[r, at, :] = dot3((high, low), (bh[o], bl[o]), NT)
+            for j in order:
+                k = (z + j) % 4
+                base = c * CHUNK + k * SUB
+                if i == 0:
+                    for d in range(2):
+                        go(part.at[r, rows(base + d * HALF, HALF)], far_in.at[r, d, k], far, (r, d, k), xdev[d])
+                elif i < 3:
+                    d = i - 1
+                    go(
+                        part.at[r, rows(base + (1 - d) * HALF, HALF)],
+                        dir_in.at[r, d, k, pl.ds((1 - d) * HALF, HALF)],
+                        dirs, (r, d, k), xdev[d],
+                    )
 
     def pass_on(r):
         for j in order:
@@ -241,33 +237,6 @@
                 remote(got, got, agx, (r, d, k), xdev[d]).wait_recv()
                 ring_relay(r, d, k).start()
 
-    def column(d, k, xx):
-        return remote(block(0, xx, k), block(0, xx, k), agc, (d, k, xx), zdev[d])
-
-    def ring_first():
-        for d in range(2):
-            got = piece(0, x + 2, z, d)
-            remote(got, got, rel, (0, d, z), xdev[d]).wait_recv()
-        for d in range(2):
-            @pl.when(z != ends[d])
-            def _(d=d):
-                for xx in range(4):
-                    column(d, z, xx).start()
-
-    def hop(*which):
-        for i in which:
-            for d in range(2):
-                k = z - i * (1 - 2 * d)
-
-                @pl.when((k >= 0) & (k <= 3))
-                def _(d=d, k=k):
-                    for xx in range(4):
-                        column(d, k, xx).wait_recv()
-
-                        @pl.when(z != ends[d])
-                        def _():
-                            column(d, k, xx).start()
-
     def arrived(r):
         for j in (0, 1, 3, 2):
             k = (z - j + 4) % 4
@@ -280,8 +249,8 @@
             at = pl.ds(pl.multiple_of(i * 128, 128), 128)
             here = full[r, at, :]
             there = full[r, :, at].T
-            th[at, :], tl[at, :] = split(2.0 * here - there)
-            uh[at, :], ul[at, :] = split(2.0 * there - here)
+            th[at, :], tl[at, :] = split(2.0 * there - here)
+            uh[at, :], ul[at, :] = split(2.0 * here - there)
             return carry
 
         lax.fori_loop(0, V // 128, step, 0)
@@ -304,14 +273,14 @@
     def density(r, first=False):
         mine = rows(a * SUB, SUB)
         amp = full[r, mine, :]
-        amp_t = 2.0 * amp - (th[mine, :].astype(F32) + tl[mine, :].astype(F32))
+        amp_t = 2.0 * amp - (uh[mine, :].astype(F32) + ul[mine, :].astype(F32))
         pad = jnp.zeros((128 - SUB, V), F32)
         amp = split(jnp.concatenate([amp, pad], axis=0))
         amp_t = split(jnp.concatenate([amp_t, pad], axis=0))
 
         for i in range(TILES):
             at = pl.ds(i * CHUNK, CHUNK)
-            value = dot3((th[at, :], tl[at, :]), amp, NT) + dot3((uh[at, :], ul[at, :]), amp_t, NT)
+            value = dot3((uh[at, :], ul[at, :]), amp, NT) + dot3((th[at, :], tl[at, :]), amp_t, NT)
             value = value.reshape(2, 2, SUB, 128)
             if first:
                 dt[2 * i : 2 * i + 2] = value
@@ -349,7 +318,7 @@
         dens_out[...] = total[0:SUB, 0:SUB]
         sent.extend([chip_copy(), far_copy()] + column_copies())
 
-    def finish(columns):
+    def finish():
         o0 = own_slot(0)
         o1 = own_slot(1)
         writes = []
@@ -363,50 +332,40 @@
             copy = pltpu.make_async_copy(gown.at[:, at], grad_hbm.at[:, at], outs.at[i])
             copy.start()
             writes.append(copy)
-            if i == 0:
-                spread(2)
         settle()
         for r in range(2):
-            remote(sendb.at[r], peer.at[r], ex, (r,), partner(r)).wait_send()
+            for i in range(5):
+                row_chunk(r, i).wait_send()
         for copy in sent:
             copy.wait_send()
         for r in range(2):
-            if r == 0 and columns:
-                continue
             for j in (1, 2, 3):
                 straight(r, j).wait_send()
             for k in range(4):
                 for d in range(2):
                     ring_block(r, d, k).wait_send()
                     ring_relay(r, d, k).wait_send()
-        if columns:
-            for d in range(2):
-                ring_block(0, d, z).wait_send()
-                ring_relay(0, d, z).wait_send()
-                for k in range(4):
-                    @pl.when(((z - k) * (1 - 2 * d) >= 0) & (z != ends[d]))
-                    def _(d=d, k=k):
-                        for xx in range(4):
-                            column(d, k, xx).wait_send()
         for copy in writes:
             copy.wait()
 
     lax.fori_loop(0, TILES, split_own, 0)
-    integral(0)
-    pass_on(0)
     before = list(sent)
 
     @pl.when(core == 0)
     def _():
         sent[:] = before
-        integral(1)
-        across(0)
+        integral(0, 0, 1)
+        integral(1, 0)
+        integral(0, 2, 3)
+        integral(1, 1, 2)
         pass_on(1)
+        integral(1, 3)
+        pass_on(0)
         across(1)
         amplitude(1)
         gather_z(1)
         gather_x(1)
-        amplitude(0)
+        across(0)
         onward(1, 1)
         relay(1, 0)
         onward(1, 3)
@@ -414,13 +373,14 @@
         onward(1, 2)
         relay(1, 3)
         relay(1, 2)
+        amplitude(0)
         arrived(1)
-        gather_z(0)
         tildes(1)
         give_back(1)
+        gather_z(0)
+        gather_x(0)
         keep(1)
         density(1, True)
-        gather_x(0)
         onward(0, 1, 3, 2)
         relay(0, 0)
         relay(0, 1)
@@ -430,47 +390,54 @@
         density(0)
         spread(0)
         give_back(0)
+        spread(1)
         keep(0)
-        spread(1)
-        finish(False)
+        spread(2)
+        finish()
 
     @pl.when(core == 1)
     def _():
         sent[:] = before
+        integral(0, 0, 1, 2, 3)
+        pass_on(0)
         exchange(1)
         across(0)
+        integral(1, 0)
         amplitude(0)
         gather_x(0)
-        integral(1)
-        relay(0, 0)
+        integral(1, 1, 2)
         pass_on(1)
+        integral(1, 3)
         across(1)
         amplitude(1)
         gather_z(1)
         gather_x(1)
+        gather_z(0)
         onward(1, 1)
         relay(1, 0)
         onward(1, 3)
         relay(1, 1)
         onward(1, 2)
-        ring_first()
-        relay(1, 3)
-        relay(1, 2)
+        relay(1, 3, 2)
+        relay(0, 0)
         arrived(1)
         tildes(1)
         give_back(1)
-        hop(1)
+        onward(0, 1, 3, 2)
+        relay(0, 1)
         keep(1)
-        hop(2)
+        relay(0, 3, 2)
         density(1, True)
-        hop(3)
+        arrived(0)
         tildes(0)
         density(0)
         spread(0)
-        give_back(0)
+        give_back(0, 0, 2)
+        spread(1)
+        give_back(0, 2, 4)
         keep(0)
-        spread(1)
-        finish(True)
+        spread(2)
+        finish()
 
 
 def body(three_index, occupied_energy, virtual_energy, plan):
@@ -518,12 +485,11 @@
             vm((4, SUB, 128), F32),
             vm((3, SUB, 128), F32),
             dma,
-            dma((2, 2)),
+            dma((2, 2, 5)),
             dma((2, 2, 2, 4)),
             dma((2, 2, 2, 4)),
             dma((2, 2, 2, 4)),
             dma((2, 2, 3)),
-            dma((2, 2, 4, 4)),
             dma((2, 2, 3)),
             dma((2, 2, 2, 4)),
             dma((2, 2, 2, 4)),

time: 132 us -> 128 us (0.970)
  Pallas kernels: 127 us -> 122 us
    pallas_call x1, Pallas kernels: 127 us -> 122 us  [body(): pl.pallas_call(kernel, out_shape=(jax.ShapeDtypeStruct((2, V, NP), F32),...]
where the time goes in v4:
time: 128 us; the launch traced here: 127 us
  Pallas kernels  122 us (95%)
  local copies, waits for them, and re-layouts  4.29 us (3%)
    pallas_call x1, Pallas kernels, body(): pl.pallas_call(kernel, out_shape=(jax.ShapeDtypeStruct((2, V, NP), F32),...  122 us
    unnamed x8, local copies, waits for them, and re-layouts  4.29 us

profile of v4, /device:TPU:1, one launch (start us, length us, event | category | flops | bytes accessed | tf_op | source)
XLA Modules:
  0.0 126.7 jit_solution(6374271183362135129)
XLA Ops:
  0.6 0.0 copy-start
  0.6 0.7 copy-done
  1.3 0.0 copy-start.1
  1.3 0.7 copy-done.1
  2.0 0.0 copy-start.2
  2.0 0.7 copy-done.2
  2.7 121.8 %pairs.1 = (f32[2,768,512]{2,1,0:T(8,128)S(1)}, f32[48,48]{1,0:T(8,128)S(1)}) custom-call(f32[2,768,512]{2,1,0:T(8,128)} %b_hbm.1, f32[2]{0:T(128)S(1)} %copy-done.2, s32[2,2]{1,0:T(2,128)S(1)} %copy-done.1, f32[768]{0:T(1024)S(1)} %copy-done), custom_call_target="tpu_custom_call" | custom-call | tf_op jit(solution)/shard_map/pairs/pallas_call | solution.py:446
  124.5 1.7 %copy.8 = f32[2,768,512]{2,1,0:T(8,128)} copy(f32[2,768,512]{2,1,0:T(8,128)S(1)} %get-tuple-element.4) | data formatting | bytes 6291456
  126.1 0.6 copy.9
Async XLA Ops:
  0.6 0.7 copy-start
  1.3 0.7 copy-start.1
  2.0 0.7 copy-start.2

commit v5 on v4

--- a/solution.py
+++ b/solution.py
@@ -371,18 +371,18 @@
         onward(1, 3)
         relay(1, 1)
         onward(1, 2)
+        amplitude(0)
+        gather_z(0)
         relay(1, 3)
         relay(1, 2)
-        amplitude(0)
+        gather_x(0)
         arrived(1)
         tildes(1)
         give_back(1)
-        gather_z(0)
-        gather_x(0)
+        onward(0, 1, 3, 2)
         keep(1)
+        relay(0, 0)
         density(1, True)
-        onward(0, 1, 3, 2)
-        relay(0, 0)
         relay(0, 1)
         relay(0, 3, 2)
         arrived(0)
@@ -420,10 +420,11 @@
         onward(1, 2)
         relay(1, 3, 2)
         relay(0, 0)
+        onward(0, 1)
         arrived(1)
         tildes(1)
         give_back(1)
-        onward(0, 1, 3, 2)
+        onward(0, 3, 2)
         relay(0, 1)
         keep(1)
         relay(0, 3, 2)

time: 128 us -> 131 us (1.023)
  the two profiles are of different devices: /device:TPU:1 before, /device:TPU:64 now
where the time goes in v5:
time: 131 us
  Pallas kernels  126 us (96%)
  local copies, waits for them, and re-layouts  4.29 us (3%)
    pallas_call x1, Pallas kernels, body(): pl.pallas_call(kernel, out_shape=(jax.ShapeDtypeStruct((2, V, NP), F32),...  126 us
    unnamed x8, local copies, waits for them, and re-layouts  4.29 us

profile of v5, /device:TPU:64, one launch (start us, length us, event | category | flops | bytes accessed | tf_op | source)
XLA Modules:
  0.0 130.8 jit_solution(10345816926617071068)
XLA Ops:
  0.6 0.0 copy-start
  0.6 0.7 copy-done
  1.3 0.0 copy-start.1
  1.3 0.7 copy-done.1
  2.0 0.0 copy-start.2
  2.0 0.7 copy-done.2
  2.7 125.9 %pairs.1 = (f32[2,768,512]{2,1,0:T(8,128)S(1)}, f32[48,48]{1,0:T(8,128)S(1)}) custom-call(f32[2,768,512]{2,1,0:T(8,128)} %b_hbm.1, f32[2]{0:T(128)S(1)} %copy-done.2, s32[2,2]{1,0:T(2,128)S(1)} %copy-done.1, f32[768]{0:T(1024)S(1)} %copy-done), custom_call_target="tpu_custom_call" | custom-call | tf_op jit(solution)/shard_map/pairs/pallas_call | solution.py:447
  128.6 1.7 %copy.8 = f32[2,768,512]{2,1,0:T(8,128)} copy(f32[2,768,512]{2,1,0:T(8,128)S(1)} %get-tuple-element.4) | data formatting | bytes 6291456
  130.2 0.6 copy.9
Async XLA Ops:
  0.6 0.7 copy-start
  1.3 0.7 copy-start.1
  2.0 0.7 copy-start.2
